TPU v7x, 512 devices: a whole 4x4x16 slice. The times are simulated.
512 devices in a mesh: ctx: 128 (over z, x, core), head: 4 (over y).
Axes of the slice: x: 4, y: 4, z: 16, core: 2. Of those that a mesh axis runs over, the one named last changes fastest.
Arguments:
- queries: bfloat16 [512, 64, 128], P('ctx', 'head'), may hold values from -24 to 24
- cache_keys: bfloat16 [32768, 8, 128], P('ctx', 'head'), may hold values from -24 to 24
- cache_values: bfloat16 [32768, 8, 128], P('ctx', 'head'), may hold values from -6 to 6
- new_keys: bfloat16 [512, 8, 128], P('ctx', 'head'), may hold values from -6 to 6
- new_values: bfloat16 [512, 8, 128], P('ctx', 'head'), may hold values from -6 to 6
- frame_of_slot: int32 [128], P('ctx'), may hold values from 0 to 127, each once
- slopes: float32 [64], P('head'), may hold values from 0.002 to 0.1
Outputs:
- attended: bfloat16 [512, 8192], P('ctx')
Inputs may be any that keep to these rules, and one draw needn't show every extreme that they name: `frame_of_slot`: each frame number 0 to 127 stands in exactly one slot.
All inputs are finite; a program needn't handle non-finite values.
Results may differ from a plain program's by a relative error of at most 0.0085.
Values may be sent and summed in bfloat16 or wider, within the bound.
No kernel may reach another device: no remote copies, remote signals or barrier semaphores. Data moves between devices by JAX's collectives and lax.ppermute only.
A program may use at most 64 MiB of HBM per device.

v0:
```python
import functools
import math

import jax
import jax.numpy as jnp
from jax import lax
from jax.experimental import pallas as pl
from jax.experimental.pallas import tpu as pltpu
from jax.sharding import Mesh, PartitionSpec as P


FRAME = 256
TAIL = 8
OFFSETS = (0, 1, -1, 2)
LOG2E = math.log2(math.e)
GRID = (16, 4, 2)
ATTEND_VMEM = 24 << 20
MERGE_VMEM = 4 << 20


def shifted(value, axis, steps):
    count = lax.axis_size(axis)
    pairs = [(source, (source + steps) % count) for source in range(count)]
    return lax.ppermute(value, axis, pairs)


def spread(value, axis):
    copies = jnp.broadcast_to(value, (lax.axis_size(axis), *value.shape))
    return lax.all_to_all(copies, axis, 0, 0)


def attend(cache_frames, kv0, kv1, kv2, kv3, q_ref, slope_ref, out_ref):
    kvs = (kv0, kv1, kv2, kv3)
    zs, rows, heads, width = q_ref.shape
    cores, _, groups, keys, _ = kv0.shape
    keys -= TAIL
    xs = len(kvs)
    group = heads // groups
    z, x, c = lax.axis_index("z"), lax.axis_index("x"), lax.axis_index("c")
    shards = [(ref, i) for ref in kvs for i in range(cores)]
    per_z = len(shards) * rows
    zb = FRAME // per_z
    zrows = rows * group
    block = zb * zrows
    scale = LOG2E / width**0.5

    row = lax.broadcasted_iota(jnp.int32, (block, width), 0)
    col = lax.broadcasted_iota(jnp.int32, (block, width), 1)
    slot = col // TAIL
    within = col % TAIL
    source = jnp.zeros_like(slot)
    for i, off in enumerate(OFFSETS):
        source = jnp.where(slot // cores == i, lax.rem(x + xs - off, xs), source)
    kpos = z * per_z + (source * cores + slot % cores) * rows + within
    real = (within < rows) & (slot < len(shards))
    lane = lax.broadcasted_iota(jnp.int32, (zrows, width), 1)
    sub = lax.broadcasted_iota(jnp.int32, (zrows, width), 0)
    tail_row = lax.broadcasted_iota(jnp.int32, (TAIL, width), 0)
    new_frame = (cache_frames + z * per_z // FRAME).astype(jnp.float32)
    filler = jnp.zeros((width - len(shards) * TAIL, width), jnp.float32)

    def tails(side, h):
        parts = [ref[a, side, h, keys:, :].astype(jnp.float32) for ref, a in shards]
        return parts, jnp.concatenate(parts + [filler], axis=0).astype(jnp.bfloat16)

    for b in range(zs // zb):
        qpos = (b * zb + row // zrows) * per_z + (x * cores + c) * rows + (row // group) % rows
        visible = real & (kpos <= qpos)
        qframe = float(cache_frames + b)
        lse_rows = jnp.zeros((zb, width), jnp.float32)
        q_all = q_ref[b * zb : (b + 1) * zb].astype(jnp.float32).reshape(zb * rows, heads, width)
        for h in range(groups):
            slope = slope_ref[h]
            q = q_all[:, h * group : (h + 1) * group, :].reshape(block, width).astype(jnp.bfloat16)
            parts, k_new = tails(0, h)
            _, v_new = tails(1, h)
            scores = []
            for part, (ref, a) in zip(parts, shards):
                bias = slope * (qframe - part[rows : rows + 1, :]) * -LOG2E
                bias = jnp.concatenate([bias] * (keys // width), axis=1)
                s = lax.dot_general(q, ref[a, 0, h, :keys, :], (((1,), (1,)), ((), ())), preferred_element_type=jnp.float32)
                t = s.reshape(block // group, group, keys) * scale + bias[None]
                scores.append(t.reshape(block, keys))
            bias = slope * (qframe - new_frame) * -LOG2E
            s = lax.dot_general(q, k_new, (((1,), (1,)), ((), ())), preferred_element_type=jnp.float32)
            t = (s.reshape(block // group, group, width) * scale + bias[None]).reshape(block, width)
            t_new = jnp.where(visible, t, -1e30)
            top = functools.reduce(jnp.maximum, scores)
            top = functools.reduce(jnp.maximum, [top[:, i : i + width] for i in range(0, keys, width)])
            high = jnp.max(jnp.maximum(top, t_new), axis=1, keepdims=True)
            total = jnp.exp2(t_new - high)
            acc = jnp.dot(total.astype(jnp.bfloat16), v_new, preferred_element_type=jnp.float32)
            for t, (ref, a) in zip(scores, shards):
                p = jnp.exp2(t - high)
                for i in range(0, keys, width):
                    total = total + p[:, i : i + width]
                acc = acc + jnp.dot(p.astype(jnp.bfloat16), ref[a, 1, h, :keys, :], preferred_element_type=jnp.float32)
            total = jnp.sum(total, axis=1, keepdims=True)
            out = (acc / total).astype(jnp.bfloat16)
            out_ref[b * zb : (b + 1) * zb, h * zrows : (h + 1) * zrows, :] = out.reshape(zb, zrows, width)
            lse = jnp.broadcast_to(high + jnp.log2(total), (block, width)).reshape(zb, zrows, width)
            lse_rows = lse_rows + jnp.sum(jnp.where((sub + h * zrows == lane)[None], lse, 0.0), axis=1)
        first = lse_rows.astype(jnp.bfloat16).astype(jnp.float32)
        second = (lse_rows - first).astype(jnp.bfloat16).astype(jnp.float32)
        third = lse_rows - first - second
        for i in range(zb):
            tail = jnp.where(tail_row == 0, first[i : i + 1], 0.0)
            tail = jnp.where(tail_row == 1, second[i : i + 1], tail)
            tail = jnp.where(tail_row == 2, third[i : i + 1], tail)
            out_ref[b * zb + i, groups * zrows :, :] = tail.astype(jnp.bfloat16)


def merge(rows, groups, in_ref, out_ref, scratch):
    zs, _, width = in_ref.shape
    count = in_ref.shape[1] - TAIL
    group = count // (rows * groups)
    lse = []
    for s in range(zs):
        tail = in_ref[s, count:, :].astype(jnp.float32)
        lse.append(tail[0:1] + tail[1:2] + tail[2:3])
    lse = jnp.concatenate(lse, axis=0)
    weight = jnp.exp2(lse - jnp.max(lse, axis=0, keepdims=True))
    weight = weight / jnp.sum(weight, axis=0, keepdims=True)
    weight = jnp.concatenate([weight, jnp.zeros((width - zs, width), jnp.float32)], axis=0).T
    acc = jnp.zeros((count, width), jnp.float32)
    for s in range(zs):
        acc = acc + weight[:count, s : s + 1] * in_ref[s, :count, :].astype(jnp.float32)
    scratch[...] = acc.reshape(groups, rows, group, width)
    for h in range(groups):
        for g in range(group):
            at = (h * group + g) * width
            out_ref[:, at : at + width] = scratch[h, :, g, :].astype(jnp.bfloat16)


def on_device(queries, cache_keys, cache_values, new_keys, new_values, frame_of_slot, slopes):
    rows, heads, width = queries.shape
    _, groups, _ = cache_keys.shape
    group = heads // groups
    zs, xs, cs = (lax.axis_size(a) for a in ("z", "x", "c"))
    cache_frames = zs * xs * cs * frame_of_slot.shape[0]
    vmem = pl.BlockSpec(memory_space=pltpu.VMEM)

    frame = jnp.broadcast_to(frame_of_slot.astype(jnp.bfloat16)[0], (groups, TAIL - rows, width))

    def side(cached, new):
        return jnp.concatenate([cached.transpose(1, 0, 2), new.transpose(1, 0, 2), frame], axis=1)

    packed = jnp.stack([side(cache_keys, new_keys), side(cache_values, new_values)])
    landing = [packed]
    for off in OFFSETS[1:]:
        landing.append(shifted(packed, "x", off))
    q_all = spread(queries, "z")
    blocks = [lax.all_gather(value, "c") for value in landing]
    slope = jnp.broadcast_to(slopes.reshape(groups, group, 1), (groups, group, width))
    chunk = groups * group * rows + TAIL
    partial = pl.pallas_call(
        functools.partial(attend, cache_frames),
        out_shape=jax.ShapeDtypeStruct((zs, chunk, width), jnp.bfloat16),
        in_specs=[vmem] * 6,
        out_specs=vmem,
        compiler_params=pltpu.CompilerParams(vmem_limit_bytes=ATTEND_VMEM),
        name="attend",
    )(*blocks, q_all, slope)
    landed = lax.all_to_all(partial, "z", 0, 0)
    result = pl.pallas_call(
        functools.partial(merge, rows, groups),
        out_shape=jax.ShapeDtypeStruct((rows, heads * width), jnp.bfloat16),
        in_specs=[vmem],
        out_specs=vmem,
        scratch_shapes=[pltpu.VMEM((groups, rows, group, width), jnp.float32)],
        compiler_params=pltpu.CompilerParams(vmem_limit_bytes=MERGE_VMEM),
        name="merge",
    )(landed)
    return jnp.concatenate(list(spread(result, "head")), axis=1)


def solution(mesh):
    heads = mesh.devices.shape[1]
    fine = Mesh(mesh.devices.reshape(*GRID, heads), ("z", "x", "c", "head"))
    ctx = ("z", "x", "c")
    return jax.shard_map(
        on_device,
        mesh=fine,
        in_specs=(P(ctx, "head", None),) * 5 + (P(ctx), P("head")),
        out_specs=P(ctx, None),
        check_vma=False,
    )
```

profile of v0, /device:TPU:2, one launch (start us, length us, event | category | flops | bytes accessed | tf_op | source)
XLA Modules:
  0.0 86.5 jit_solution(16608574943426505892)
XLA Ops:
  0.0 1.5 %broadcast_in_dim.17 = bf16[16,4,16,128]{3,2,1,0:T(8,128)(2,1)} broadcast(bf16[4,16,128]{2,1,0:T(8,128)(2,1)} %param.7), dimensions={1,2,3} | broadcast | bytes 278528 | tf_op jit(solution)/shard_map/broadcast_in_dim | solution.py:28
  1.5 0.0 copy-start
  1.5 0.0 copy-start.1
  1.5 15.3 %all-to-all-start = ((bf16[16,4,16,128]{3,2,1,0:T(8,128)(2,1)}), bf16[16,4,16,128]{3,2,1,0:T(8,128)(2,1)S(1)}, u32[]{:S(2)}, u32[]{:S(2)}) async-start(bf16[16,4,16,128]{3,2,1,0:T(8,128)(2,1)} %broadcast_in_dim.17), calls=%async_computation | async-start | bytes 524288 | tf_op jit(solution)/shard_map/all_to_all | solution.py:29
  17.5 0.0 copy-start.3
  17.5 0.0 copy-start.2
  17.5 0.1 pad.11.clone
  17.6 0.6 copy-done.3
  18.1 0.0 copy-done.2
  18.2 0.0 copy-done
  18.2 0.0 copy-done.1
  18.2 0.1 maximum_bitcast_fusion
  18.3 0.0 copy-start.4
  18.4 4.0 %collective-permute-start.2 = (bf16[2,2,264,128]{3,2,1,0:T(8,128)(2,1)S(1)}, bf16[2,2,264,128]{3,2,1,0:T(8,128)(2,1)S(1)}, u32[]{:S(2)}, u32[]{:S(2)}) collective-permute-start(bf16[2,2,264,128]{3,2,1,0:T(8,128)(2,1)S(1)} %pad_maximum_fusion), channel_id=1, source_target_pairs={{0,16},{8,24},{16,0},{24,8},{1,17},{9,25},{17,1},{25,9},{2,18},{10... | collective-permute-start | bytes 811016 | tf_op jit(solution)/shard_map/ppermute | solution.py:24
  22.4 3.3 %collective-permute-start.1 = (bf16[2,2,264,128]{3,2,1,0:T(8,128)(2,1)S(1)}, bf16[2,2,264,128]{3,2,1,0:T(8,128)(2,1)S(1)}, u32[]{:S(2)}, u32[]{:S(2)}) collective-permute-start(bf16[2,2,264,128]{3,2,1,0:T(8,128)(2,1)S(1)} %pad_maximum_fusion), channel_id=1, source_target_pairs={{0,24},{8,0},{16,8},{24,16},{1,25},{9,1},{17,9},{25,17},{2,26},{10... | collective-permute-start | bytes 811016 | tf_op jit(solution)/shard_map/ppermute | solution.py:24
  25.8 2.5 %collective-permute-start = (bf16[2,2,264,128]{3,2,1,0:T(8,128)(2,1)S(1)}, bf16[2,2,264,128]{3,2,1,0:T(8,128)(2,1)S(1)}, u32[]{:S(2)}, u32[]{:S(2)}) collective-permute-start(bf16[2,2,264,128]{3,2,1,0:T(8,128)(2,1)S(1)} %pad_maximum_fusion), channel_id=1, source_target_pairs={{0,8},{8,16},{16,24},{24,0},{1,9},{9,17},{17,25},{25,1},{2,10},{10... | collective-permute-start | bytes 811016 | tf_op jit(solution)/shard_map/ppermute | solution.py:24
  28.3 0.0 copy-done.4
  28.3 0.1 broadcast_in_dim.18
  28.4 2.2 %all-gather = bf16[4,2,264,128]{3,2,1,0:T(8,128)(2,1)S(1)} all-gather(bf16[2,2,264,128]{3,2,1,0:T(8,128)(2,1)S(1)} %pad_maximum_fusion), channel_id=2, replica_groups=mesh['z'=16,'x'=4,'c'=2,'head'=4] {'c'}, dimensions={0}, use_global_device_ids=true | all-gather | bytes 811008 | tf_op jit(solution)/shard_map/all_gather | solution.py:153
  30.6 0.6 collective-permute-done.2
  31.2 2.2 %all-gather.3 = bf16[4,2,264,128]{3,2,1,0:T(8,128)(2,1)S(1)} all-gather(bf16[2,2,264,128]{3,2,1,0:T(8,128)(2,1)S(1)} %collective-permute-done.2), channel_id=5, replica_groups=mesh['z'=16,'x'=4,'c'=2,'head'=4] {'c'}, dimensions={0}, use_global_device_ids=true | all-gather | bytes 811008 | tf_op jit(solution)/shard_map/all_gather | solution.py:153
  33.4 2.2 %collective-permute-done.1 = bf16[2,2,264,128]{3,2,1,0:T(8,128)(2,1)S(1)} collective-permute-done((bf16[2,2,264,128]{3,2,1,0:T(8,128)(2,1)S(1)}, bf16[2,2,264,128]{3,2,1,0:T(8,128)(2,1)S(1)}, u32[]{:S(2)}, u32[]{:S(2)}) %collective-permute-start.1) | collective-permute-done | bytes 270368 | tf_op jit(solution)/shard_map/ppermute | solution.py:24
  35.5 2.2 %all-gather.2 = bf16[4,2,264,128]{3,2,1,0:T(8,128)(2,1)S(1)} all-gather(bf16[2,2,264,128]{3,2,1,0:T(8,128)(2,1)S(1)} %collective-permute-done.1), channel_id=4, replica_groups=mesh['z'=16,'x'=4,'c'=2,'head'=4] {'c'}, dimensions={0}, use_global_device_ids=true | all-gather | bytes 811008 | tf_op jit(solution)/shard_map/all_gather | solution.py:153
  37.7 0.0 collective-permute-done
  37.7 2.2 %all-gather.1 = bf16[4,2,264,128]{3,2,1,0:T(8,128)(2,1)S(1)} all-gather(bf16[2,2,264,128]{3,2,1,0:T(8,128)(2,1)S(1)} %collective-permute-done), channel_id=3, replica_groups=mesh['z'=16,'x'=4,'c'=2,'head'=4] {'c'}, dimensions={0}, use_global_device_ids=true | all-gather | bytes 811008 | tf_op jit(solution)/shard_map/all_gather | solution.py:153
  39.9 0.0 all-to-all-done.q_ref
  39.9 0.1 broadcast_in_dim.19.slope_ref
  40.0 4.0 %attend.1 = bf16[16,72,128]{2,1,0:T(8,128)(2,1)S(1)} custom-call(bf16[2,2,2,264,128]{4,3,2,1,0:T(8,128)(2,1)S(1)} %bitcast.25, bf16[2,2,2,264,128]{4,3,2,1,0:T(8,128)(2,1)S(1)} %bitcast.28, bf16[2,2,2,264,128]{4,3,2,1,0:T(8,128)(2,1)S(1)} %bitcast.27, bf16[2,2,2,264,128]{4,3,2,1,0:T(8,128)(2,1)S(1)} %bitcast.26, ...), custom_call_target="tpu_custom_call" | custom-call | tf_op jit(solution)/shard_map/attend/pallas_call | solution.py:156
  44.0 31.4 %all_to_all.15.in_ref = bf16[16,72,128]{2,1,0:T(8,128)(2,1)S(1)} all-to-all(bf16[16,72,128]{2,1,0:T(8,128)(2,1)S(1)} %attend.1), channel_id=1, replica_groups=mesh['z'=16,'x'=4,'c'=2,'head'=4] {'z'}, dimensions={0} | all-to-all | bytes 589824 | tf_op jit(solution)/shard_map/all_to_all | solution.py:164
  75.5 0.4 merge.1
  75.9 9.9 %all_to_all.16 = bf16[4,4,2048]{2,1,0:T(4,128)(2,1)S(1)} all-to-all(bf16[4,4,2048]{2,1,0:T(4,128)(2,1)S(1)} %broadcast_in_dim.20), channel_id=1, replica_groups=mesh['z'=16,'x'=4,'c'=2,'head'=4] {'head'}, dimensions={0} | all-to-all | bytes 131072 | tf_op jit(solution)/shard_map/all_to_all | solution.py:29
  85.8 0.7 pad_maximum_fusion.1
  (6 shorter events, 0.1 us)
Async XLA Ops:
  1.5 16.7 %copy-start = (bf16[256,2,128]{2,1,0:T(2,128)(2,1)S(1)}, bf16[256,2,128]{2,1,0:T(2,128)(2,1)}, u32[]{:S(2)}) copy-start(bf16[256,2,128]{2,1,0:T(2,128)(2,1)} %param.9) | copy-start | bytes 393220
  1.5 16.7 %copy-start.1 = (bf16[256,2,128]{2,1,0:T(2,128)(2,1)S(1)}, bf16[256,2,128]{2,1,0:T(2,128)(2,1)}, u32[]{:S(2)}) copy-start(bf16[256,2,128]{2,1,0:T(2,128)(2,1)} %param.8) | copy-start | bytes 393220
  1.5 38.4 %all-to-all-start = ((bf16[16,4,16,128]{3,2,1,0:T(8,128)(2,1)}), bf16[16,4,16,128]{3,2,1,0:T(8,128)(2,1)S(1)}, u32[]{:S(2)}, u32[]{:S(2)}) async-start(bf16[16,4,16,128]{3,2,1,0:T(8,128)(2,1)} %broadcast_in_dim.17), calls=%async_computation | async-start | bytes 524288 | tf_op jit(solution)/shard_map/all_to_all | solution.py:29
  17.5 0.7 copy-start.3
  17.5 0.7 copy-start.2
  18.3 9.9 %copy-start.4 = (f32[16]{0:T(128)S(1)}, f32[16]{0:T(128)}, u32[]{:S(2)}) copy-start(f32[16]{0:T(128)} %param.13) | copy-start | bytes 196
  18.4 12.8 %collective-permute-start.2 = (bf16[2,2,264,128]{3,2,1,0:T(8,128)(2,1)S(1)}, bf16[2,2,264,128]{3,2,1,0:T(8,128)(2,1)S(1)}, u32[]{:S(2)}, u32[]{:S(2)}) collective-permute-start(bf16[2,2,264,128]{3,2,1,0:T(8,128)(2,1)S(1)} %pad_maximum_fusion), channel_id=1, source_target_pairs={{0,16},{8,24},{16,0},{24,8},{1,17},{9,25},{17,1},{25,9},{2,18},{10... | collective-permute-start | bytes 811016 | tf_op jit(solution)/shard_map/ppermute | solution.py:24
  22.4 13.1 %collective-permute-start.1 = (bf16[2,2,264,128]{3,2,1,0:T(8,128)(2,1)S(1)}, bf16[2,2,264,128]{3,2,1,0:T(8,128)(2,1)S(1)}, u32[]{:S(2)}, u32[]{:S(2)}) collective-permute-start(bf16[2,2,264,128]{3,2,1,0:T(8,128)(2,1)S(1)} %pad_maximum_fusion), channel_id=1, source_target_pairs={{0,24},{8,0},{16,8},{24,16},{1,25},{9,1},{17,9},{25,17},{2,26},{10... | collective-permute-start | bytes 811016 | tf_op jit(solution)/shard_map/ppermute | solution.py:24
  25.8 11.9 %collective-permute-start = (bf16[2,2,264,128]{3,2,1,0:T(8,128)(2,1)S(1)}, bf16[2,2,264,128]{3,2,1,0:T(8,128)(2,1)S(1)}, u32[]{:S(2)}, u32[]{:S(2)}) collective-permute-start(bf16[2,2,264,128]{3,2,1,0:T(8,128)(2,1)S(1)} %pad_maximum_fusion), channel_id=1, source_target_pairs={{0,8},{8,16},{16,24},{24,0},{1,9},{9,17},{17,25},{25,1},{2,10},{10... | collective-permute-start | bytes 811016 | tf_op jit(solution)/shard_map/ppermute | solution.py:24
where the time goes:
time: 87 us; the launch traced here: 86.5 us
  blocking collectives  50.1 us (58%)
  starting transfers between devices  25.2 us (29%)
  Pallas kernels  4.45 us (5%)
  waiting for transfers between devices  2.78 us (3%)
  local copies, waits for them, and re-layouts  2.39 us (3%)
    all_to_all x1, blocking collectives, on_device(): landed = lax.all_to_all(partial, 'z', 0, 0)  31.4 us
    all_to_all x1, starting transfers between devices, spread(): return lax.all_to_all(copies, axis, 0, 0)  15.3 us
    all_to_all x1, blocking collectives, spread(): return lax.all_to_all(copies, axis, 0, 0)  9.88 us
    ppermute x3, starting transfers between devices, shifted(): return lax.ppermute(value, axis, pairs)  9.88 us
    all_gather x4, blocking collectives, on_device(): blocks = [lax.all_gather(value, 'c') for value in landing]  8.72 us
    pallas_call x1, Pallas kernels, on_device(): pl.pallas_call(functools.partial(attend, cache_frames), out_shape=jax.Sha...  4.04 us
    ppermute x3, waiting for transfers between devices, shifted(): return lax.ppermute(value, axis, pairs)  2.78 us
  transfers between devices with their start and end apart: 4, of which 2 were waited for; matrix products, arithmetic and copies ran while one was open for 0% of the time, Pallas kernels for 0%

commit v1 on v0

--- a/solution.py
+++ b/solution.py
@@ -14,6 +14,8 @@
 OFFSETS = (0, 1, -1, 2)
 LOG2E = math.log2(math.e)
 GRID = (16, 4, 2)
+Q_FIRST = 10
+OUT_FIRST = 2
 ATTEND_VMEM = 24 << 20
 MERGE_VMEM = 4 << 20
 
@@ -24,9 +26,14 @@
     return lax.ppermute(value, axis, pairs)
 
 
-def spread(value, axis):
+def ring(axis, first):
+    count = lax.axis_size(axis)
+    return [(first + i) % count for i in range(count)]
+
+
+def spread(value, axis, first=0):
     copies = jnp.broadcast_to(value, (lax.axis_size(axis), *value.shape))
-    return lax.all_to_all(copies, axis, 0, 0)
+    return lax.all_to_all(copies, axis, 0, 0, axis_index_groups=[ring(axis, first)])
 
 
 def attend(cache_frames, kv0, kv1, kv2, kv3, q_ref, slope_ref, out_ref):
@@ -68,7 +75,9 @@
         visible = real & (kpos <= qpos)
         qframe = float(cache_frames + b)
         lse_rows = jnp.zeros((zb, width), jnp.float32)
-        q_all = q_ref[b * zb : (b + 1) * zb].astype(jnp.float32).reshape(zb * rows, heads, width)
+        q_at = [(b * zb + i - Q_FIRST) % zs for i in range(zb)]
+        out_at = [(b * zb + i - OUT_FIRST) % zs for i in range(zb)]
+        q_all = jnp.concatenate([q_ref[i].astype(jnp.float32) for i in q_at], axis=0)
         for h in range(groups):
             slope = slope_ref[h]
             q = q_all[:, h * group : (h + 1) * group, :].reshape(block, width).astype(jnp.bfloat16)
@@ -97,17 +106,18 @@
                 acc = acc + jnp.dot(p.astype(jnp.bfloat16), ref[a, 1, h, :keys, :], preferred_element_type=jnp.float32)
             total = jnp.sum(total, axis=1, keepdims=True)
             out = (acc / total).astype(jnp.bfloat16)
-            out_ref[b * zb : (b + 1) * zb, h * zrows : (h + 1) * zrows, :] = out.reshape(zb, zrows, width)
+            for i, at in enumerate(out_at):
+                out_ref[at, h * zrows : (h + 1) * zrows, :] = out[i * zrows : (i + 1) * zrows, :]
             lse = jnp.broadcast_to(high + jnp.log2(total), (block, width)).reshape(zb, zrows, width)
             lse_rows = lse_rows + jnp.sum(jnp.where((sub + h * zrows == lane)[None], lse, 0.0), axis=1)
         first = lse_rows.astype(jnp.bfloat16).astype(jnp.float32)
         second = (lse_rows - first).astype(jnp.bfloat16).astype(jnp.float32)
         third = lse_rows - first - second
-        for i in range(zb):
+        for i, at in enumerate(out_at):
             tail = jnp.where(tail_row == 0, first[i : i + 1], 0.0)
             tail = jnp.where(tail_row == 1, second[i : i + 1], tail)
             tail = jnp.where(tail_row == 2, third[i : i + 1], tail)
-            out_ref[b * zb + i, groups * zrows :, :] = tail.astype(jnp.bfloat16)
+            out_ref[at, groups * zrows :, :] = tail.astype(jnp.bfloat16)
 
 
 def merge(rows, groups, in_ref, out_ref, scratch):
@@ -149,7 +159,7 @@
     landing = [packed]
     for off in OFFSETS[1:]:
         landing.append(shifted(packed, "x", off))
-    q_all = spread(queries, "z")
+    q_all = spread(queries, "z", Q_FIRST)
     blocks = [lax.all_gather(value, "c") for value in landing]
     slope = jnp.broadcast_to(slopes.reshape(groups, group, 1), (groups, group, width))
     chunk = groups * group * rows + TAIL
@@ -161,7 +171,7 @@
         compiler_params=pltpu.CompilerParams(vmem_limit_bytes=ATTEND_VMEM),
         name="attend",
     )(*blocks, q_all, slope)
-    landed = lax.all_to_all(partial, "z", 0, 0)
+    landed = lax.all_to_all(partial, "z", 0, 0, axis_index_groups=[ring("z", OUT_FIRST)])
     result = pl.pallas_call(
         functools.partial(merge, rows, groups),
         out_shape=jax.ShapeDtypeStruct((rows, heads * width), jnp.bfloat16),

time: 87 us -> 83.3 us (0.957)
  the two profiles are of different devices: /device:TPU:2 before, /device:TPU:32 now
where the time goes in v1:
time: 83.3 us; the launch traced here: 82.8 us
  blocking collectives  45.2 us (54%)
  starting transfers between devices  27.5 us (33%)
  Pallas kernels  4.44 us (5%)
  local copies, waits for them, and re-layouts  2.39 us (3%)
  waiting for transfers between devices  1.69 us (2%)
    all_to_all x1, blocking collectives, on_device(): lax.all_to_all(partial, 'z', 0, 0, axis_index_groups=[ring('z', OUT_FIRST)])  26.5 us
    all_to_all x1, starting transfers between devices, spread(): lax.all_to_all(copies, axis, 0, 0, axis_index_groups=[ring(axis, first)])  16.7 us
    ppermute x3, starting transfers between devices, shifted(): return lax.ppermute(value, axis, pairs)  10.8 us
    all_to_all x1, blocking collectives, spread(): lax.all_to_all(copies, axis, 0, 0, axis_index_groups=[ring(axis, first)])  9.89 us
    all_gather x4, blocking collectives, on_device(): blocks = [lax.all_gather(value, 'c') for value in landing]  8.72 us
    pallas_call x1, Pallas kernels, on_device(): pl.pallas_call(functools.partial(attend, cache_frames), out_shape=jax.Sha...  4.04 us
    ppermute x3, waiting for transfers between devices, shifted(): return lax.ppermute(value, axis, pairs)  1.69 us
  transfers between devices with their start and end apart: 4, of which 1 were waited for; matrix products, arithmetic and copies ran while one was open for 0% of the time, Pallas kernels for 0%

profile of v1, /device:TPU:32, one launch (start us, length us, event | category | flops | bytes accessed | tf_op | source)
XLA Modules:
  0.0 82.8 jit_solution(3371326549428262550)
XLA Ops:
  0.0 1.5 %broadcast_in_dim.17 = bf16[16,4,16,128]{3,2,1,0:T(8,128)(2,1)} broadcast(bf16[4,16,128]{2,1,0:T(8,128)(2,1)} %param.7), dimensions={1,2,3} | broadcast | bytes 278528 | tf_op jit(solution)/shard_map/broadcast_in_dim | solution.py:35
  1.5 0.0 copy-start
  1.5 0.0 copy-start.1
  1.5 16.7 %all-to-all-start = ((bf16[16,4,16,128]{3,2,1,0:T(8,128)(2,1)}), bf16[16,4,16,128]{3,2,1,0:T(8,128)(2,1)S(1)}, u32[]{:S(2)}, u32[]{:S(2)}) async-start(bf16[16,4,16,128]{3,2,1,0:T(8,128)(2,1)} %broadcast_in_dim.17), calls=%async_computation | async-start | bytes 524288 | tf_op jit(solution)/shard_map/all_to_all | solution.py:36
  18.9 0.0 copy-start.3
  18.9 0.0 copy-start.2
  18.9 0.1 pad.11.clone
  19.0 0.6 copy-done.3
  19.5 0.0 copy-done.2
  19.6 0.0 copy-done
  19.6 0.0 copy-done.1
  19.6 0.1 maximum_bitcast_fusion
  19.7 0.0 copy-start.4
  19.8 4.9 %collective-permute-start.2 = (bf16[2,2,264,128]{3,2,1,0:T(8,128)(2,1)S(1)}, bf16[2,2,264,128]{3,2,1,0:T(8,128)(2,1)S(1)}, u32[]{:S(2)}, u32[]{:S(2)}) collective-permute-start(bf16[2,2,264,128]{3,2,1,0:T(8,128)(2,1)S(1)} %pad_maximum_fusion), channel_id=1, source_target_pairs={{0,16},{8,24},{16,0},{24,8},{1,17},{9,25},{17,1},{25,9},{2,18},{10... | collective-permute-start | bytes 811016 | tf_op jit(solution)/shard_map/ppermute | solution.py:26
  24.7 3.0 %collective-permute-start.1 = (bf16[2,2,264,128]{3,2,1,0:T(8,128)(2,1)S(1)}, bf16[2,2,264,128]{3,2,1,0:T(8,128)(2,1)S(1)}, u32[]{:S(2)}, u32[]{:S(2)}) collective-permute-start(bf16[2,2,264,128]{3,2,1,0:T(8,128)(2,1)S(1)} %pad_maximum_fusion), channel_id=1, source_target_pairs={{0,24},{8,0},{16,8},{24,16},{1,25},{9,1},{17,9},{25,17},{2,26},{10... | collective-permute-start | bytes 811016 | tf_op jit(solution)/shard_map/ppermute | solution.py:26
  27.8 2.8 %collective-permute-start = (bf16[2,2,264,128]{3,2,1,0:T(8,128)(2,1)S(1)}, bf16[2,2,264,128]{3,2,1,0:T(8,128)(2,1)S(1)}, u32[]{:S(2)}, u32[]{:S(2)}) collective-permute-start(bf16[2,2,264,128]{3,2,1,0:T(8,128)(2,1)S(1)} %pad_maximum_fusion), channel_id=1, source_target_pairs={{0,8},{8,16},{16,24},{24,0},{1,9},{9,17},{17,25},{25,1},{2,10},{10... | collective-permute-start | bytes 811016 | tf_op jit(solution)/shard_map/ppermute | solution.py:26
  30.6 0.0 copy-done.4
  30.6 0.1 broadcast_in_dim.18
  30.7 2.2 %all-gather = bf16[4,2,264,128]{3,2,1,0:T(8,128)(2,1)S(1)} all-gather(bf16[2,2,264,128]{3,2,1,0:T(8,128)(2,1)S(1)} %pad_maximum_fusion), channel_id=2, replica_groups=mesh['z'=16,'x'=4,'c'=2,'head'=4] {'c'}, dimensions={0}, use_global_device_ids=true | all-gather | bytes 811008 | tf_op jit(solution)/shard_map/all_gather | solution.py:163
  32.9 0.0 collective-permute-done.2
  32.9 2.2 %all-gather.3 = bf16[4,2,264,128]{3,2,1,0:T(8,128)(2,1)S(1)} all-gather(bf16[2,2,264,128]{3,2,1,0:T(8,128)(2,1)S(1)} %collective-permute-done.2), channel_id=5, replica_groups=mesh['z'=16,'x'=4,'c'=2,'head'=4] {'c'}, dimensions={0}, use_global_device_ids=true | all-gather | bytes 811008 | tf_op jit(solution)/shard_map/all_gather | solution.py:163
  35.1 1.7 %collective-permute-done.1 = bf16[2,2,264,128]{3,2,1,0:T(8,128)(2,1)S(1)} collective-permute-done((bf16[2,2,264,128]{3,2,1,0:T(8,128)(2,1)S(1)}, bf16[2,2,264,128]{3,2,1,0:T(8,128)(2,1)S(1)}, u32[]{:S(2)}, u32[]{:S(2)}) %collective-permute-start.1) | collective-permute-done | bytes 270368 | tf_op jit(solution)/shard_map/ppermute | solution.py:26
  36.7 2.2 %all-gather.2 = bf16[4,2,264,128]{3,2,1,0:T(8,128)(2,1)S(1)} all-gather(bf16[2,2,264,128]{3,2,1,0:T(8,128)(2,1)S(1)} %collective-permute-done.1), channel_id=4, replica_groups=mesh['z'=16,'x'=4,'c'=2,'head'=4] {'c'}, dimensions={0}, use_global_device_ids=true | all-gather | bytes 811008 | tf_op jit(solution)/shard_map/all_gather | solution.py:163
  38.9 0.0 collective-permute-done
  38.9 2.2 %all-gather.1 = bf16[4,2,264,128]{3,2,1,0:T(8,128)(2,1)S(1)} all-gather(bf16[2,2,264,128]{3,2,1,0:T(8,128)(2,1)S(1)} %collective-permute-done), channel_id=3, replica_groups=mesh['z'=16,'x'=4,'c'=2,'head'=4] {'c'}, dimensions={0}, use_global_device_ids=true | all-gather | bytes 811008 | tf_op jit(solution)/shard_map/all_gather | solution.py:163
  41.1 0.0 all-to-all-done.q_ref
  41.1 0.1 broadcast_in_dim.19.slope_ref
  41.2 4.0 %attend.1 = bf16[16,72,128]{2,1,0:T(8,128)(2,1)S(1)} custom-call(bf16[2,2,2,264,128]{4,3,2,1,0:T(8,128)(2,1)S(1)} %bitcast.25, bf16[2,2,2,264,128]{4,3,2,1,0:T(8,128)(2,1)S(1)} %bitcast.28, bf16[2,2,2,264,128]{4,3,2,1,0:T(8,128)(2,1)S(1)} %bitcast.27, bf16[2,2,2,264,128]{4,3,2,1,0:T(8,128)(2,1)S(1)} %bitcast.26, ...), custom_call_target="tpu_custom_call" | custom-call | tf_op jit(solution)/shard_map/attend/pallas_call | solution.py:166
  45.2 26.5 %all_to_all.15.in_ref = bf16[16,72,128]{2,1,0:T(8,128)(2,1)S(1)} all-to-all(bf16[16,72,128]{2,1,0:T(8,128)(2,1)S(1)} %attend.1), channel_id=1, replica_groups={{64,96,128,160,192,224,256,288,320,352,384,416,448,480,0,32},{65,97,129..., dimensions={0} | all-to-all | bytes 589824 | tf_op jit(solution)/shard_map/all_to_all | solution.py:174
  71.8 0.4 merge.1
  72.2 9.9 %all_to_all.16 = bf16[4,4,2048]{2,1,0:T(4,128)(2,1)S(1)} all-to-all(bf16[4,4,2048]{2,1,0:T(4,128)(2,1)S(1)} %broadcast_in_dim.20), channel_id=1, replica_groups={{0,1,2,3},{4,5,6,7},{8,9,10,11},{12,13,14,15},{16,17,18,19},{20,21,22,2..., dimensions={0} | all-to-all | bytes 131072 | tf_op jit(solution)/shard_map/all_to_all | solution.py:36
  82.1 0.7 pad_maximum_fusion.1
  (6 shorter events, 0.1 us)
Async XLA Ops:
  1.5 18.1 %copy-start = (bf16[256,2,128]{2,1,0:T(2,128)(2,1)S(1)}, bf16[256,2,128]{2,1,0:T(2,128)(2,1)}, u32[]{:S(2)}) copy-start(bf16[256,2,128]{2,1,0:T(2,128)(2,1)} %param.9) | copy-start | bytes 393220
  1.5 18.1 %copy-start.1 = (bf16[256,2,128]{2,1,0:T(2,128)(2,1)S(1)}, bf16[256,2,128]{2,1,0:T(2,128)(2,1)}, u32[]{:S(2)}) copy-start(bf16[256,2,128]{2,1,0:T(2,128)(2,1)} %param.8) | copy-start | bytes 393220
  1.5 39.6 %all-to-all-start = ((bf16[16,4,16,128]{3,2,1,0:T(8,128)(2,1)}), bf16[16,4,16,128]{3,2,1,0:T(8,128)(2,1)S(1)}, u32[]{:S(2)}, u32[]{:S(2)}) async-start(bf16[16,4,16,128]{3,2,1,0:T(8,128)(2,1)} %broadcast_in_dim.17), calls=%async_computation | async-start | bytes 524288 | tf_op jit(solution)/shard_map/all_to_all | solution.py:36
  18.9 0.7 copy-start.3
  18.9 0.7 copy-start.2
  19.7 10.8 %copy-start.4 = (f32[16]{0:T(128)S(1)}, f32[16]{0:T(128)}, u32[]{:S(2)}) copy-start(f32[16]{0:T(128)} %param.13) | copy-start | bytes 196
  19.8 13.1 %collective-permute-start.2 = (bf16[2,2,264,128]{3,2,1,0:T(8,128)(2,1)S(1)}, bf16[2,2,264,128]{3,2,1,0:T(8,128)(2,1)S(1)}, u32[]{:S(2)}, u32[]{:S(2)}) collective-permute-start(bf16[2,2,264,128]{3,2,1,0:T(8,128)(2,1)S(1)} %pad_maximum_fusion), channel_id=1, source_target_pairs={{0,16},{8,24},{16,0},{24,8},{1,17},{9,25},{17,1},{25,9},{2,18},{10... | collective-permute-start | bytes 811016 | tf_op jit(solution)/shard_map/ppermute | solution.py:26
  24.7 12.0 %collective-permute-start.1 = (bf16[2,2,264,128]{3,2,1,0:T(8,128)(2,1)S(1)}, bf16[2,2,264,128]{3,2,1,0:T(8,128)(2,1)S(1)}, u32[]{:S(2)}, u32[]{:S(2)}) collective-permute-start(bf16[2,2,264,128]{3,2,1,0:T(8,128)(2,1)S(1)} %pad_maximum_fusion), channel_id=1, source_target_pairs={{0,24},{8,0},{16,8},{24,16},{1,25},{9,1},{17,9},{25,17},{2,26},{10... | collective-permute-start | bytes 811016 | tf_op jit(solution)/shard_map/ppermute | solution.py:26
  27.8 11.1 %collective-permute-start = (bf16[2,2,264,128]{3,2,1,0:T(8,128)(2,1)S(1)}, bf16[2,2,264,128]{3,2,1,0:T(8,128)(2,1)S(1)}, u32[]{:S(2)}, u32[]{:S(2)}) collective-permute-start(bf16[2,2,264,128]{3,2,1,0:T(8,128)(2,1)S(1)} %pad_maximum_fusion), channel_id=1, source_target_pairs={{0,8},{8,16},{16,24},{24,0},{1,9},{9,17},{17,25},{25,1},{2,10},{10... | collective-permute-start | bytes 811016 | tf_op jit(solution)/shard_map/ppermute | solution.py:26

commit v2 on v1

--- a/solution.py
+++ b/solution.py
@@ -11,11 +11,12 @@
 
 FRAME = 256
 TAIL = 8
-OFFSETS = (0, 1, -1, 2)
+OFFSETS = (0, -1, 1, 2)
 LOG2E = math.log2(math.e)
 GRID = (16, 4, 2)
-Q_FIRST = 10
-OUT_FIRST = 2
+Q_FIRST = 8
+OUT_FIRST = 0
+HEAD_FIRST = 3
 ATTEND_VMEM = 24 << 20
 MERGE_VMEM = 4 << 20
 
@@ -181,7 +182,8 @@
         compiler_params=pltpu.CompilerParams(vmem_limit_bytes=MERGE_VMEM),
         name="merge",
     )(landed)
-    return jnp.concatenate(list(spread(result, "head")), axis=1)
+    parts = spread(result, "head", HEAD_FIRST)
+    return jnp.concatenate([parts[ring("head", HEAD_FIRST).index(i)] for i in range(len(parts))], axis=1)
 
 
 def solution(mesh):

time: 83.3 us -> 80.9 us (0.971)
  the two profiles are of different devices: /device:TPU:32 before, /device:TPU:24 now
where the time goes in v2:
time: 80.9 us; the launch traced here: 79.5 us
  blocking collectives  39.6 us (49%)
  starting transfers between devices  31 us (38%)
  Pallas kernels  4.44 us (5%)
  local copies, waits for them, and re-layouts  2.39 us (3%)
  other arithmetic  0.81 us (1%)
    all_to_all x1, blocking collectives, on_device(): lax.all_to_all(partial, 'z', 0, 0, axis_index_groups=[ring('z', OUT_FIRST)])  22.8 us
    all_to_all x1, starting transfers between devices, spread(): lax.all_to_all(copies, axis, 0, 0, axis_index_groups=[ring(axis, first)])  19 us
    ppermute x3, starting transfers between devices, shifted(): return lax.ppermute(value, axis, pairs)  12 us
    all_gather x4, blocking collectives, on_device(): blocks = [lax.all_gather(value, 'c') for value in landing]  8.72 us
    all_to_all x1, blocking collectives, spread(): lax.all_to_all(copies, axis, 0, 0, axis_index_groups=[ring(axis, first)])  7.99 us
    pallas_call x1, Pallas kernels, on_device(): pl.pallas_call(functools.partial(attend, cache_frames), out_shape=jax.Sha...  4.04 us
  transfers between devices with their start and end apart: 4, of which 1 were waited for; matrix products, arithmetic and copies ran while one was open for 0% of the time, Pallas kernels for 0%

profile of v2, /device:TPU:24, one launch (start us, length us, event | category | flops | bytes accessed | tf_op | source)
XLA Modules:
  0.0 79.5 jit_solution(12132183509764927232)
XLA Ops:
  0.0 1.5 %broadcast_in_dim.17 = bf16[16,4,16,128]{3,2,1,0:T(8,128)(2,1)} broadcast(bf16[4,16,128]{2,1,0:T(8,128)(2,1)} %param.7), dimensions={1,2,3} | broadcast | bytes 278528 | tf_op jit(solution)/shard_map/broadcast_in_dim | solution.py:36
  1.5 0.0 copy-start
  1.5 0.0 copy-start.1
  1.5 19.0 %all-to-all-start = ((bf16[16,4,16,128]{3,2,1,0:T(8,128)(2,1)}), bf16[16,4,16,128]{3,2,1,0:T(8,128)(2,1)S(1)}, u32[]{:S(2)}, u32[]{:S(2)}) async-start(bf16[16,4,16,128]{3,2,1,0:T(8,128)(2,1)} %broadcast_in_dim.17), calls=%async_computation | async-start | bytes 524288 | tf_op jit(solution)/shard_map/all_to_all | solution.py:37
  21.1 0.0 copy-start.3
  21.1 0.0 copy-start.2
  21.1 0.1 pad.11.clone
  21.2 0.6 copy-done.3
  21.8 0.0 copy-done.2
  21.8 0.0 copy-done
  21.8 0.0 copy-done.1
  21.9 0.1 maximum_bitcast_fusion
  22.0 0.0 copy-start.4
  22.0 4.9 %collective-permute-start.2 = (bf16[2,2,264,128]{3,2,1,0:T(8,128)(2,1)S(1)}, bf16[2,2,264,128]{3,2,1,0:T(8,128)(2,1)S(1)}, u32[]{:S(2)}, u32[]{:S(2)}) collective-permute-start(bf16[2,2,264,128]{3,2,1,0:T(8,128)(2,1)S(1)} %pad_maximum_fusion), channel_id=1, source_target_pairs={{0,16},{8,24},{16,0},{24,8},{1,17},{9,25},{17,1},{25,9},{2,18},{10... | collective-permute-start | bytes 811016 | tf_op jit(solution)/shard_map/ppermute | solution.py:27
  27.0 2.5 %collective-permute-start.1 = (bf16[2,2,264,128]{3,2,1,0:T(8,128)(2,1)S(1)}, bf16[2,2,264,128]{3,2,1,0:T(8,128)(2,1)S(1)}, u32[]{:S(2)}, u32[]{:S(2)}) collective-permute-start(bf16[2,2,264,128]{3,2,1,0:T(8,128)(2,1)S(1)} %pad_maximum_fusion), channel_id=1, source_target_pairs={{0,8},{8,16},{16,24},{24,0},{1,9},{9,17},{17,25},{25,1},{2,10},{10... | collective-permute-start | bytes 811016 | tf_op jit(solution)/shard_map/ppermute | solution.py:27
  29.5 4.6 %collective-permute-start = (bf16[2,2,264,128]{3,2,1,0:T(8,128)(2,1)S(1)}, bf16[2,2,264,128]{3,2,1,0:T(8,128)(2,1)S(1)}, u32[]{:S(2)}, u32[]{:S(2)}) collective-permute-start(bf16[2,2,264,128]{3,2,1,0:T(8,128)(2,1)S(1)} %pad_maximum_fusion), channel_id=1, source_target_pairs={{0,24},{8,0},{16,8},{24,16},{1,25},{9,1},{17,9},{25,17},{2,26},{10... | collective-permute-start | bytes 811016 | tf_op jit(solution)/shard_map/ppermute | solution.py:27
  34.1 0.0 copy-done.4
  34.1 0.1 broadcast_in_dim.18
  34.1 2.2 %all-gather = bf16[4,2,264,128]{3,2,1,0:T(8,128)(2,1)S(1)} all-gather(bf16[2,2,264,128]{3,2,1,0:T(8,128)(2,1)S(1)} %pad_maximum_fusion), channel_id=2, replica_groups=mesh['z'=16,'x'=4,'c'=2,'head'=4] {'c'}, dimensions={0}, use_global_device_ids=true | all-gather | bytes 811008 | tf_op jit(solution)/shard_map/all_gather | solution.py:164
  36.3 0.0 collective-permute-done.2
  36.3 2.2 %all-gather.3 = bf16[4,2,264,128]{3,2,1,0:T(8,128)(2,1)S(1)} all-gather(bf16[2,2,264,128]{3,2,1,0:T(8,128)(2,1)S(1)} %collective-permute-done.2), channel_id=5, replica_groups=mesh['z'=16,'x'=4,'c'=2,'head'=4] {'c'}, dimensions={0}, use_global_device_ids=true | all-gather | bytes 811008 | tf_op jit(solution)/shard_map/all_gather | solution.py:164
  38.5 0.5 collective-permute-done.1
  39.0 2.2 %all-gather.2 = bf16[4,2,264,128]{3,2,1,0:T(8,128)(2,1)S(1)} all-gather(bf16[2,2,264,128]{3,2,1,0:T(8,128)(2,1)S(1)} %collective-permute-done.1), channel_id=4, replica_groups=mesh['z'=16,'x'=4,'c'=2,'head'=4] {'c'}, dimensions={0}, use_global_device_ids=true | all-gather | bytes 811008 | tf_op jit(solution)/shard_map/all_gather | solution.py:164
  41.2 0.0 collective-permute-done
  41.2 2.2 %all-gather.1 = bf16[4,2,264,128]{3,2,1,0:T(8,128)(2,1)S(1)} all-gather(bf16[2,2,264,128]{3,2,1,0:T(8,128)(2,1)S(1)} %collective-permute-done), channel_id=3, replica_groups=mesh['z'=16,'x'=4,'c'=2,'head'=4] {'c'}, dimensions={0}, use_global_device_ids=true | all-gather | bytes 811008 | tf_op jit(solution)/shard_map/all_gather | solution.py:164
  43.4 0.0 all-to-all-done.q_ref
  43.4 0.1 broadcast_in_dim.19.slope_ref
  43.5 4.0 %attend.1 = bf16[16,72,128]{2,1,0:T(8,128)(2,1)S(1)} custom-call(bf16[2,2,2,264,128]{4,3,2,1,0:T(8,128)(2,1)S(1)} %bitcast.25, bf16[2,2,2,264,128]{4,3,2,1,0:T(8,128)(2,1)S(1)} %bitcast.28, bf16[2,2,2,264,128]{4,3,2,1,0:T(8,128)(2,1)S(1)} %bitcast.27, bf16[2,2,2,264,128]{4,3,2,1,0:T(8,128)(2,1)S(1)} %bitcast.26, ...), custom_call_target="tpu_custom_call" | custom-call | tf_op jit(solution)/shard_map/attend/pallas_call | solution.py:167
  47.5 22.8 %all_to_all.15.in_ref = bf16[16,72,128]{2,1,0:T(8,128)(2,1)S(1)} all-to-all(bf16[16,72,128]{2,1,0:T(8,128)(2,1)S(1)} %attend.1), channel_id=1, replica_groups={{0,32,64,96,128,160,192,224,256,288,320,352,384,416,448,480},{1,33,65,9..., dimensions={0} | all-to-all | bytes 589824 | tf_op jit(solution)/shard_map/all_to_all | solution.py:175
  70.4 0.4 merge.1
  70.8 8.0 %all_to_all.16 = bf16[4,4,2048]{2,1,0:T(4,128)(2,1)S(1)} all-to-all(bf16[4,4,2048]{2,1,0:T(4,128)(2,1)S(1)} %broadcast_in_dim.20), channel_id=1, replica_groups={{3,0,1,2},{7,4,5,6},{11,8,9,10},{15,12,13,14},{19,16,17,18},{23,20,21,2..., dimensions={0} | all-to-all | bytes 131072 | tf_op jit(solution)/shard_map/all_to_all | solution.py:37
  78.8 0.7 pad_maximum_fusion.1
  (6 shorter events, 0.1 us)
Async XLA Ops:
  1.5 20.4 %copy-start = (bf16[256,2,128]{2,1,0:T(2,128)(2,1)S(1)}, bf16[256,2,128]{2,1,0:T(2,128)(2,1)}, u32[]{:S(2)}) copy-start(bf16[256,2,128]{2,1,0:T(2,128)(2,1)} %param.9) | copy-start | bytes 393220
  1.5 20.4 %copy-start.1 = (bf16[256,2,128]{2,1,0:T(2,128)(2,1)S(1)}, bf16[256,2,128]{2,1,0:T(2,128)(2,1)}, u32[]{:S(2)}) copy-start(bf16[256,2,128]{2,1,0:T(2,128)(2,1)} %param.8) | copy-start | bytes 393220
  1.5 41.9 %all-to-all-start = ((bf16[16,4,16,128]{3,2,1,0:T(8,128)(2,1)}), bf16[16,4,16,128]{3,2,1,0:T(8,128)(2,1)S(1)}, u32[]{:S(2)}, u32[]{:S(2)}) async-start(bf16[16,4,16,128]{3,2,1,0:T(8,128)(2,1)} %broadcast_in_dim.17), calls=%async_computation | async-start | bytes 524288 | tf_op jit(solution)/shard_map/all_to_all | solution.py:37
  21.1 0.7 copy-start.3
  21.1 0.7 copy-start.2
  22.0 12.1 %copy-start.4 = (f32[16]{0:T(128)S(1)}, f32[16]{0:T(128)}, u32[]{:S(2)}) copy-start(f32[16]{0:T(128)} %param.13) | copy-start | bytes 196
  22.0 14.3 %collective-permute-start.2 = (bf16[2,2,264,128]{3,2,1,0:T(8,128)(2,1)S(1)}, bf16[2,2,264,128]{3,2,1,0:T(8,128)(2,1)S(1)}, u32[]{:S(2)}, u32[]{:S(2)}) collective-permute-start(bf16[2,2,264,128]{3,2,1,0:T(8,128)(2,1)S(1)} %pad_maximum_fusion), channel_id=1, source_target_pairs={{0,16},{8,24},{16,0},{24,8},{1,17},{9,25},{17,1},{25,9},{2,18},{10... | collective-permute-start | bytes 811016 | tf_op jit(solution)/shard_map/ppermute | solution.py:27
  27.0 12.0 %collective-permute-start.1 = (bf16[2,2,264,128]{3,2,1,0:T(8,128)(2,1)S(1)}, bf16[2,2,264,128]{3,2,1,0:T(8,128)(2,1)S(1)}, u32[]{:S(2)}, u32[]{:S(2)}) collective-permute-start(bf16[2,2,264,128]{3,2,1,0:T(8,128)(2,1)S(1)} %pad_maximum_fusion), channel_id=1, source_target_pairs={{0,8},{8,16},{16,24},{24,0},{1,9},{9,17},{17,25},{25,1},{2,10},{10... | collective-permute-start | bytes 811016 | tf_op jit(solution)/shard_map/ppermute | solution.py:27
  29.5 11.7 %collective-permute-start = (bf16[2,2,264,128]{3,2,1,0:T(8,128)(2,1)S(1)}, bf16[2,2,264,128]{3,2,1,0:T(8,128)(2,1)S(1)}, u32[]{:S(2)}, u32[]{:S(2)}) collective-permute-start(bf16[2,2,264,128]{3,2,1,0:T(8,128)(2,1)S(1)} %pad_maximum_fusion), channel_id=1, source_target_pairs={{0,24},{8,0},{16,8},{24,16},{1,25},{9,1},{17,9},{25,17},{2,26},{10... | collective-permute-start | bytes 811016 | tf_op jit(solution)/shard_map/ppermute | solution.py:27

commit v3 on v2

--- a/solution.py
+++ b/solution.py
@@ -14,9 +14,9 @@
 OFFSETS = (0, -1, 1, 2)
 LOG2E = math.log2(math.e)
 GRID = (16, 4, 2)
-Q_FIRST = 8
-OUT_FIRST = 0
-HEAD_FIRST = 3
+Q_FIRST = 9
+OUT_FIRST = 15
+HEAD_FIRST = 1
 ATTEND_VMEM = 24 << 20
 MERGE_VMEM = 4 << 20
 

time: 80.9 us -> 80.7 us (level)
  the two profiles are of different devices: /device:TPU:24 before, /device:TPU:2 now
where the time goes in v3:
time: 80.7 us; the launch traced here: 80.2 us
  blocking collectives  41.3 us (51%)
  starting transfers between devices  28 us (35%)
  Pallas kernels  4.44 us (6%)
  waiting for transfers between devices  2.57 us (3%)
  local copies, waits for them, and re-layouts  2.39 us (3%)
  other arithmetic  0.81 us (1%)
    all_to_all x1, blocking collectives, on_device(): lax.all_to_all(partial, 'z', 0, 0, axis_index_groups=[ring('z', OUT_FIRST)])  23 us
    all_to_all x1, starting transfers between devices, spread(): lax.all_to_all(copies, axis, 0, 0, axis_index_groups=[ring(axis, first)])  18.1 us
    ppermute x3, starting transfers between devices, shifted(): return lax.ppermute(value, axis, pairs)  9.88 us
    all_to_all x1, blocking collectives, spread(): lax.all_to_all(copies, axis, 0, 0, axis_index_groups=[ring(axis, first)])  9.54 us
    all_gather x4, blocking collectives, on_device(): blocks = [lax.all_gather(value, 'c') for value in landing]  8.72 us
    pallas_call x1, Pallas kernels, on_device(): pl.pallas_call(functools.partial(attend, cache_frames), out_shape=jax.Sha...  4.03 us
    ppermute x3, waiting for transfers between devices, shifted(): return lax.ppermute(value, axis, pairs)  2.57 us
  transfers between devices with their start and end apart: 4, of which 1 were waited for; matrix products, arithmetic and copies ran while one was open for 0% of the time, Pallas kernels for 0%

profile of v3, /device:TPU:2, one launch (start us, length us, event | category | flops | bytes accessed | tf_op | source)
XLA Modules:
  0.0 80.2 jit_solution(4471599314674790621)
XLA Ops:
  0.0 1.5 %broadcast_in_dim.17 = bf16[16,4,16,128]{3,2,1,0:T(8,128)(2,1)} broadcast(bf16[4,16,128]{2,1,0:T(8,128)(2,1)} %param.7), dimensions={1,2,3} | broadcast | bytes 278528 | tf_op jit(solution)/shard_map/broadcast_in_dim | solution.py:36
  1.5 0.0 copy-start
  1.5 0.0 copy-start.1
  1.5 18.1 %all-to-all-start = ((bf16[16,4,16,128]{3,2,1,0:T(8,128)(2,1)}), bf16[16,4,16,128]{3,2,1,0:T(8,128)(2,1)S(1)}, u32[]{:S(2)}, u32[]{:S(2)}) async-start(bf16[16,4,16,128]{3,2,1,0:T(8,128)(2,1)} %broadcast_in_dim.17), calls=%async_computation | async-start | bytes 524288 | tf_op jit(solution)/shard_map/all_to_all | solution.py:37
  20.2 0.0 copy-start.3
  20.2 0.0 copy-start.2
  20.2 0.1 pad.11.clone
  20.3 0.6 copy-done.3
  20.9 0.0 copy-done.2
  20.9 0.0 copy-done
  20.9 0.0 copy-done.1
  21.0 0.1 maximum_bitcast_fusion
  21.1 0.0 copy-start.4
  21.1 4.0 %collective-permute-start.2 = (bf16[2,2,264,128]{3,2,1,0:T(8,128)(2,1)S(1)}, bf16[2,2,264,128]{3,2,1,0:T(8,128)(2,1)S(1)}, u32[]{:S(2)}, u32[]{:S(2)}) collective-permute-start(bf16[2,2,264,128]{3,2,1,0:T(8,128)(2,1)S(1)} %pad_maximum_fusion), channel_id=1, source_target_pairs={{0,16},{8,24},{16,0},{24,8},{1,17},{9,25},{17,1},{25,9},{2,18},{10... | collective-permute-start | bytes 811016 | tf_op jit(solution)/shard_map/ppermute | solution.py:27
  25.2 1.9 %collective-permute-start.1 = (bf16[2,2,264,128]{3,2,1,0:T(8,128)(2,1)S(1)}, bf16[2,2,264,128]{3,2,1,0:T(8,128)(2,1)S(1)}, u32[]{:S(2)}, u32[]{:S(2)}) collective-permute-start(bf16[2,2,264,128]{3,2,1,0:T(8,128)(2,1)S(1)} %pad_maximum_fusion), channel_id=1, source_target_pairs={{0,8},{8,16},{16,24},{24,0},{1,9},{9,17},{17,25},{25,1},{2,10},{10... | collective-permute-start | bytes 811016 | tf_op jit(solution)/shard_map/ppermute | solution.py:27
  27.1 3.9 %collective-permute-start = (bf16[2,2,264,128]{3,2,1,0:T(8,128)(2,1)S(1)}, bf16[2,2,264,128]{3,2,1,0:T(8,128)(2,1)S(1)}, u32[]{:S(2)}, u32[]{:S(2)}) collective-permute-start(bf16[2,2,264,128]{3,2,1,0:T(8,128)(2,1)S(1)} %pad_maximum_fusion), channel_id=1, source_target_pairs={{0,24},{8,0},{16,8},{24,16},{1,25},{9,1},{17,9},{25,17},{2,26},{10... | collective-permute-start | bytes 811016 | tf_op jit(solution)/shard_map/ppermute | solution.py:27
  31.0 0.0 copy-done.4
  31.1 0.1 broadcast_in_dim.18
  31.1 2.2 %all-gather = bf16[4,2,264,128]{3,2,1,0:T(8,128)(2,1)S(1)} all-gather(bf16[2,2,264,128]{3,2,1,0:T(8,128)(2,1)S(1)} %pad_maximum_fusion), channel_id=2, replica_groups=mesh['z'=16,'x'=4,'c'=2,'head'=4] {'c'}, dimensions={0}, use_global_device_ids=true | all-gather | bytes 811008 | tf_op jit(solution)/shard_map/all_gather | solution.py:164
  33.3 0.0 collective-permute-done.2
  33.3 2.2 %all-gather.3 = bf16[4,2,264,128]{3,2,1,0:T(8,128)(2,1)S(1)} all-gather(bf16[2,2,264,128]{3,2,1,0:T(8,128)(2,1)S(1)} %collective-permute-done.2), channel_id=5, replica_groups=mesh['z'=16,'x'=4,'c'=2,'head'=4] {'c'}, dimensions={0}, use_global_device_ids=true | all-gather | bytes 811008 | tf_op jit(solution)/shard_map/all_gather | solution.py:164
  35.5 2.6 %collective-permute-done.1 = bf16[2,2,264,128]{3,2,1,0:T(8,128)(2,1)S(1)} collective-permute-done((bf16[2,2,264,128]{3,2,1,0:T(8,128)(2,1)S(1)}, bf16[2,2,264,128]{3,2,1,0:T(8,128)(2,1)S(1)}, u32[]{:S(2)}, u32[]{:S(2)}) %collective-permute-start.1) | collective-permute-done | bytes 270368 | tf_op jit(solution)/shard_map/ppermute | solution.py:27
  38.1 2.2 %all-gather.2 = bf16[4,2,264,128]{3,2,1,0:T(8,128)(2,1)S(1)} all-gather(bf16[2,2,264,128]{3,2,1,0:T(8,128)(2,1)S(1)} %collective-permute-done.1), channel_id=4, replica_groups=mesh['z'=16,'x'=4,'c'=2,'head'=4] {'c'}, dimensions={0}, use_global_device_ids=true | all-gather | bytes 811008 | tf_op jit(solution)/shard_map/all_gather | solution.py:164
  40.3 0.0 collective-permute-done
  40.3 2.2 %all-gather.1 = bf16[4,2,264,128]{3,2,1,0:T(8,128)(2,1)S(1)} all-gather(bf16[2,2,264,128]{3,2,1,0:T(8,128)(2,1)S(1)} %collective-permute-done), channel_id=3, replica_groups=mesh['z'=16,'x'=4,'c'=2,'head'=4] {'c'}, dimensions={0}, use_global_device_ids=true | all-gather | bytes 811008 | tf_op jit(solution)/shard_map/all_gather | solution.py:164
  42.4 0.0 all-to-all-done.q_ref
  42.4 0.1 broadcast_in_dim.19.slope_ref
  42.5 4.0 %attend.1 = bf16[16,72,128]{2,1,0:T(8,128)(2,1)S(1)} custom-call(bf16[2,2,2,264,128]{4,3,2,1,0:T(8,128)(2,1)S(1)} %bitcast.25, bf16[2,2,2,264,128]{4,3,2,1,0:T(8,128)(2,1)S(1)} %bitcast.28, bf16[2,2,2,264,128]{4,3,2,1,0:T(8,128)(2,1)S(1)} %bitcast.27, bf16[2,2,2,264,128]{4,3,2,1,0:T(8,128)(2,1)S(1)} %bitcast.26, ...), custom_call_target="tpu_custom_call" | custom-call | tf_op jit(solution)/shard_map/attend/pallas_call | solution.py:167
  46.5 23.0 %all_to_all.15.in_ref = bf16[16,72,128]{2,1,0:T(8,128)(2,1)S(1)} all-to-all(bf16[16,72,128]{2,1,0:T(8,128)(2,1)S(1)} %attend.1), channel_id=1, replica_groups={{480,0,32,64,96,128,160,192,224,256,288,320,352,384,416,448},{481,1,33,..., dimensions={0} | all-to-all | bytes 589824 | tf_op jit(solution)/shard_map/all_to_all | solution.py:175
  69.5 0.4 merge.1
  70.0 9.5 %all_to_all.16 = bf16[4,4,2048]{2,1,0:T(4,128)(2,1)S(1)} all-to-all(bf16[4,4,2048]{2,1,0:T(4,128)(2,1)S(1)} %broadcast_in_dim.20), channel_id=1, replica_groups={{1,2,3,0},{5,6,7,4},{9,10,11,8},{13,14,15,12},{17,18,19,16},{21,22,23,2..., dimensions={0} | all-to-all | bytes 131072 | tf_op jit(solution)/shard_map/all_to_all | solution.py:37
  79.6 0.7 pad_maximum_fusion.1
  (6 shorter events, 0.1 us)
Async XLA Ops:
  1.5 19.5 %copy-start = (bf16[256,2,128]{2,1,0:T(2,128)(2,1)S(1)}, bf16[256,2,128]{2,1,0:T(2,128)(2,1)}, u32[]{:S(2)}) copy-start(bf16[256,2,128]{2,1,0:T(2,128)(2,1)} %param.9) | copy-start | bytes 393220
  1.5 19.5 %copy-start.1 = (bf16[256,2,128]{2,1,0:T(2,128)(2,1)S(1)}, bf16[256,2,128]{2,1,0:T(2,128)(2,1)}, u32[]{:S(2)}) copy-start(bf16[256,2,128]{2,1,0:T(2,128)(2,1)} %param.8) | copy-start | bytes 393220
  1.5 41.0 %all-to-all-start = ((bf16[16,4,16,128]{3,2,1,0:T(8,128)(2,1)}), bf16[16,4,16,128]{3,2,1,0:T(8,128)(2,1)S(1)}, u32[]{:S(2)}, u32[]{:S(2)}) async-start(bf16[16,4,16,128]{3,2,1,0:T(8,128)(2,1)} %broadcast_in_dim.17), calls=%async_computation | async-start | bytes 524288 | tf_op jit(solution)/shard_map/all_to_all | solution.py:37
  20.2 0.7 copy-start.3
  20.2 0.7 copy-start.2
  21.1 9.9 %copy-start.4 = (f32[16]{0:T(128)S(1)}, f32[16]{0:T(128)}, u32[]{:S(2)}) copy-start(f32[16]{0:T(128)} %param.13) | copy-start | bytes 196
  21.1 12.2 %collective-permute-start.2 = (bf16[2,2,264,128]{3,2,1,0:T(8,128)(2,1)S(1)}, bf16[2,2,264,128]{3,2,1,0:T(8,128)(2,1)S(1)}, u32[]{:S(2)}, u32[]{:S(2)}) collective-permute-start(bf16[2,2,264,128]{3,2,1,0:T(8,128)(2,1)S(1)} %pad_maximum_fusion), channel_id=1, source_target_pairs={{0,16},{8,24},{16,0},{24,8},{1,17},{9,25},{17,1},{25,9},{2,18},{10... | collective-permute-start | bytes 811016 | tf_op jit(solution)/shard_map/ppermute | solution.py:27
  25.2 12.9 %collective-permute-start.1 = (bf16[2,2,264,128]{3,2,1,0:T(8,128)(2,1)S(1)}, bf16[2,2,264,128]{3,2,1,0:T(8,128)(2,1)S(1)}, u32[]{:S(2)}, u32[]{:S(2)}) collective-permute-start(bf16[2,2,264,128]{3,2,1,0:T(8,128)(2,1)S(1)} %pad_maximum_fusion), channel_id=1, source_target_pairs={{0,8},{8,16},{16,24},{24,0},{1,9},{9,17},{17,25},{25,1},{2,10},{10... | collective-permute-start | bytes 811016 | tf_op jit(solution)/shard_map/ppermute | solution.py:27
  27.1 13.1 %collective-permute-start = (bf16[2,2,264,128]{3,2,1,0:T(8,128)(2,1)S(1)}, bf16[2,2,264,128]{3,2,1,0:T(8,128)(2,1)S(1)}, u32[]{:S(2)}, u32[]{:S(2)}) collective-permute-start(bf16[2,2,264,128]{3,2,1,0:T(8,128)(2,1)S(1)} %pad_maximum_fusion), channel_id=1, source_target_pairs={{0,24},{8,0},{16,8},{24,16},{1,25},{9,1},{17,9},{25,17},{2,26},{10... | collective-permute-start | bytes 811016 | tf_op jit(solution)/shard_map/ppermute | solution.py:27
